TPU v7x, 32 devices: a whole 2x2x4 slice. The times are simulated.
32 devices in a mesh: segment: 2 (over x), blk: 16 (over z, y, core).
Axes of the slice: x: 2, y: 2, z: 4, core: 2. Of those that a mesh axis runs over, the one named last changes fastest.
Arguments:
- pixels: bfloat16 [128, 4, 2048], P('segment', None, 'blk'), may hold values from -6 to 6
- var_group: int32 [128], P('segment'), may hold values from 0 to 7
- var_embed: bfloat16 [128, 2048], P('segment'), may hold values from -3 to 3
- group_weight: bfloat16 [8, 4, 2048], replicated, may hold values from -3 to 3
- agg_query: bfloat16 [2048], replicated, may hold values from -180 to 180
- lat_index: int32 [2048], P('blk'), may hold values from 0 to 359
- lat_table: bfloat16 [360, 2048], replicated, may hold values from -6 to 6
- norm_gain: float32 [2048], replicated, may hold values from 0.1 to 1.9
- w_query: bfloat16 [2048, 1024], P(None, 'segment'), may hold values from -9 to 9
- w_key: bfloat16 [2048, 1024], P(None, 'segment'), may hold values from -0.125 to 0.125
- w_value: bfloat16 [2048, 1024], P(None, 'segment'), may hold values from -0.125 to 0.125
- w_out: bfloat16 [1024, 2048], P('segment'), may hold values from -1.796875 to 1.796875
Outputs:
- aggregated: bfloat16 [2048, 2048], P('blk', 'segment')
- attended: bfloat16 [2048, 2048], P('blk', 'segment')
All inputs are finite; a program needn't handle non-finite values.
Results may differ from a plain program's by a relative error of at most 0.015.
The roundings to bfloat16 on the way count: a program that leaves them out, or rounds other values in their place, can miss the bound.
Values may be sent and summed in bfloat16 or wider, within the bound.
A program may use at most 64 MiB of HBM per device.

v0:
```python
import math
import jax
import jax.numpy as jnp
from jax import lax
from jax.sharding import PartitionSpec as P

HEAD_DIM = 128


def merged(part, axis, combine):
    gathered = jax.tree.map(lambda a: lax.all_gather(a, axis), part)

    def take(source):
        return jax.tree.map(lambda a: lax.dynamic_index_in_dim(a, source, 0, False), gathered)

    return lax.fori_loop(
        1, lax.axis_size(axis), lambda source, state: combine(state, take(source)), take(0)
    )


def combine_parts(first, second):
    peak = jnp.maximum(first[0], second[0])
    scale_first = jnp.exp(first[0] - peak)
    scale_second = jnp.exp(second[0] - peak)
    total = first[1] * scale_first + second[1] * scale_second
    summed = first[2] * scale_first[:, None] + second[2] * scale_second[:, None]
    return (peak, total, summed)


def on_device(
    pixels,
    var_group,
    var_embed,
    group_weight,
    agg_query,
    lat_index,
    lat_table,
    norm_gain,
    w_query,
    w_key,
    w_value,
    w_out,
):
    highest = lax.Precision.HIGHEST
    width = var_embed.shape[1]
    groups = group_weight.shape[0]
    tok_rows = pixels.shape[2]
    lat_rows = lat_table.shape[0]
    sections = lax.axis_size("segment")
    share = width // sections
    start = lax.axis_index("segment") * share
    query32 = agg_query.astype(jnp.float32)
    group32 = group_weight.astype(jnp.float32)
    embed32 = var_embed.astype(jnp.float32)
    pixel32 = pixels.astype(jnp.float32)
    proj_group = jnp.einsum("gpd,d->gp", group32, query32, precision=highest)
    onehot = (var_group[:, None] == jnp.arange(groups, dtype=jnp.int32)[None, :]).astype(
        jnp.float32
    )
    proj_var = jnp.dot(onehot, proj_group, precision=highest)
    offset = jnp.dot(embed32, query32, precision=highest)
    scores = (
        jnp.einsum("vpt,vp->vt", pixel32, proj_var, precision=highest) + offset[:, None]
    ) / math.sqrt(width)
    lat_hot = (lat_index[:, None] == jnp.arange(lat_rows, dtype=jnp.int32)[None, :]).astype(
        jnp.bfloat16
    )
    local_peak = jnp.max(scores, axis=0)
    expo = jnp.exp(scores - local_peak[None, :])
    total = jnp.sum(expo, axis=0)
    grouped = jnp.einsum("vg,vpt->gpt", onehot, expo[:, None, :] * pixel32, precision=highest)
    summed = jnp.einsum("vt,vd->td", expo, embed32, precision=highest)
    summed = summed + jnp.einsum("gpt,gpd->td", grouped, group32, precision=highest)
    local_total = total
    local_sum = summed
    peak, total, summed = merged((local_peak, local_total, local_sum), "segment", combine_parts)
    lat_part = jnp.dot(lat_hot, lat_table, preferred_element_type=jnp.float32)
    latent = summed / total[:, None] + lat_part
    center = latent - jnp.mean(latent, axis=1, keepdims=True)
    spread = jnp.mean(center * center, axis=1, keepdims=True)
    normed = (center * lax.rsqrt(spread + 1e-05) * norm_gain[None, :]).astype(jnp.bfloat16)
    latent_share = lax.dynamic_slice_in_dim(latent, start, share, 1)
    aggregated = latent_share.astype(jnp.bfloat16)
    queries = jnp.dot(normed, w_query, preferred_element_type=jnp.float32).astype(jnp.bfloat16)
    keys = jnp.dot(normed, w_key, preferred_element_type=jnp.float32).astype(jnp.bfloat16)
    values = jnp.dot(normed, w_value, preferred_element_type=jnp.float32).astype(jnp.bfloat16)
    head_count = queries.shape[1] // HEAD_DIM
    query_heads = queries.reshape(tok_rows, head_count, HEAD_DIM)
    scale = 1.0 / math.sqrt(HEAD_DIM)

    def attend(carry, key_heads, value_heads):
        running, total, accum = carry
        logits = (
            jnp.einsum("thd,rhd->thr", query_heads, key_heads, preferred_element_type=jnp.float32)
            * scale
        )
        fresh = jnp.maximum(running, jnp.max(logits, axis=2))
        shrink = jnp.exp(running - fresh)
        expo = jnp.exp(logits - fresh[:, :, None])
        total = total * shrink + jnp.sum(expo, axis=2)
        mixed = jnp.einsum(
            "thr,rhd->thd",
            expo.astype(jnp.bfloat16),
            value_heads,
            preferred_element_type=jnp.float32,
        )
        accum = accum * shrink[:, :, None] + mixed
        return (fresh, total, accum)

    start_state = (
        jnp.full((tok_rows, head_count), -1e30, jnp.float32),
        jnp.zeros((tok_rows, head_count), jnp.float32),
        jnp.zeros((tok_rows, head_count, HEAD_DIM), jnp.float32),
    )
    carry = start_state
    key_rows = lax.all_gather(keys, "blk", axis=0, tiled=True)
    value_rows = lax.all_gather(values, "blk", axis=0, tiled=True)
    rows = key_rows.shape[0]
    block = 2048
    key_blocks = key_rows.reshape(rows // block, block, head_count, HEAD_DIM)
    value_blocks = value_rows.reshape(rows // block, block, head_count, HEAD_DIM)

    def one_block(state, blocks):
        return (attend(state, blocks[0], blocks[1]), None)

    carry, unused = lax.scan(one_block, carry, (key_blocks, value_blocks))
    running, total, accum = carry
    heads_out = (
        (accum / total[:, :, None]).reshape(tok_rows, head_count * HEAD_DIM).astype(jnp.bfloat16)
    )
    partial_value = jnp.dot(heads_out, w_out, preferred_element_type=jnp.float32)
    attended = lax.psum_scatter(
        partial_value.astype(jnp.bfloat16), "segment", scatter_dimension=1, tiled=True
    )
    return (aggregated, attended)


def solution(mesh):
    in_specs = (
        P("segment", None, "blk"),
        P("segment"),
        P("segment", None),
        P(),
        P(),
        P("blk"),
        P(),
        P(),
        P(None, "segment"),
        P(None, "segment"),
        P(None, "segment"),
        P("segment", None),
    )
    out_specs = (P("blk", "segment"), P("blk", "segment"))
    return jax.shard_map(
        on_device, mesh=mesh, in_specs=in_specs, out_specs=out_specs, check_vma=False
    )
```

profile of v0, /device:TPU:0, one launch (start us, length us, event | category | flops | bytes accessed | tf_op | source)
XLA Modules:
  0.0 174.4 jit_solution(17387931946372268658)
XLA Ops:
  7.2 0.0 copy-start
  7.2 0.0 copy-start.4
  7.2 0.0 all-gather.13.cloned.1.call-start
  7.2 0.9 reshape.118
  8.1 0.7 reshape.114
  8.8 1.1 convolution_bitcast_fusion.1
  9.9 1.6 fusion.48
  11.5 0.9 fusion.32
  12.4 1.2 fusion.49
  13.6 0.1 fusion.34
  13.7 0.1 fusion.46
  13.8 0.9 convert_multiply_fusion
  14.7 0.9 fusion.27
  15.6 0.0 copy-start.6
  15.6 1.5 convolution_bitcast_fusion
  17.1 0.0 copy-done.4
  17.1 1.6 convolution_add_fusion.1
  18.8 0.0 all-gather.13.cloned.1.call-update
  18.8 0.0 all-gather.9.cloned.1.call-start
  18.8 5.2 %all-gather.4 = f32[2,1,128]{2,1,0:T(1,128)S(1)} all-gather(f32[1,1,128]{2,1,0:T(1,128)S(1)} %bitcast.113), channel_id=4, replica_groups=mesh['segment'=2,'blk'=16] {'segment'}, dimensions={0}, use_global_device_ids=true | all-gather | bytes 1536 | tf_op jit(solution)/shard_map/all_gather | solution.py:11
  24.0 4.2 %all-gather.3 = f32[2,1,128]{2,1,0:T(1,128)S(1)} all-gather(f32[1,1,128]{2,1,0:T(1,128)S(1)} %bitcast.112), channel_id=3, replica_groups=mesh['segment'=2,'blk'=16] {'segment'}, dimensions={0}, use_global_device_ids=true | all-gather | bytes 1536 | tf_op jit(solution)/shard_map/all_gather | solution.py:11
  28.2 26.5 %all-gather.13.cloned.1.call-done = f32[256,2048]{1,0:T(8,128)} async-done(((f32[128,2048]{1,0:T(8,128)}), f32[256,2048]{1,0:T(8,128)}) %all-gather.13.cloned.1.call-update) | async-done | bytes 2097168 | tf_op jit(solution)/shard_map/all_gather | solution.py:11
  54.8 0.0 copy-done.6
  54.8 0.0 copy-start.5
  54.8 2.6 %fusion.47 = (f32[128]{0:T(128)S(1)}, f32[128,2048]{1,0:T(8,128)S(1)}) fusion(bf16[360,2048]{1,0:T(8,128)(2,1)} %param.18, s32[128]{0:T(128)S(1)} %copy-done.6, f32[128]{0:T(128)S(1)} %get-tuple-element.33, f32[128]{0:T(128)S(1)} %get-tuple-element.35, f32[256,2048]{1,0:T(8,128)} %all-gather.13.cloned.1.call-done, f32[128]{0:T(128)S(1)} %get-tuple-element.34), kind=kOutput, calls=%fused_computation.65 | convolution fusion | flops 190362496 | bytes 4622848 | tf_op jit(solution)/shard_map/dot_general | solution.py:77
  57.4 0.0 copy-start.2
  57.4 0.0 copy-start.3
  57.4 0.3 multiply_reduce_fusion
  57.6 0.8 copy-done.2
  58.4 0.0 copy-done.5
  58.4 0.2 multiply_convert_fusion
  58.6 0.7 copy-done.3
  59.3 1.1 convolution_convert_fusion.3
  60.4 0.0 all-gather.9.cloned.1.call-update
  60.5 0.0 all-gather.11.cloned.1.call-start
  60.5 2.7 %convolution_convert_fusion.1 = bf16[128,512]{1,0:T(8,128)(2,1)} fusion(bf16[128,2048]{1,0:T(8,128)(2,1)S(1)} %multiply_convert_fusion, bf16[2048,512]{1,0:T(8,128)(2,1)} %param.22), kind=kOutput, calls=%fused_computation.17 | convolution fusion | flops 268500992 | bytes 2752512 | tf_op jit(solution)/shard_map/dot_general | solution.py:86
  63.2 0.0 all-gather.11.cloned.1.call-update
  63.2 0.0 reduce-scatter.2.cloned.1.call-start
  63.3 2.0 %fusion.16 = bf16[16,4,8,128]{3,2,1,0:T(8,128)(2,1)S(1)} fusion(bf16[128,2048]{1,0:T(8,128)(2,1)S(1)} %multiply_convert_fusion, bf16[2048,512]{1,0:T(8,128)(2,1)} %param.20), kind=kOutput, calls=%fused_computation.20 | convolution fusion | flops 268500992 | bytes 2752512 | tf_op jit(solution)/shard_map/dot_general | solution.py:84
  65.3 36.8 %all-gather.9.cloned.1.call-done = bf16[2048,512]{1,0:T(8,128)(2,1)} async-done(((bf16[128,512]{1,0:T(8,128)(2,1)}), bf16[2048,512]{1,0:T(8,128)(2,1)}) %all-gather.9.cloned.1.call-update) | async-done | bytes 2097168 | tf_op jit(solution)/shard_map/all_gather | solution.py:116
  102.1 2.3 %bitcast_reduce_fusion = (f32[128,4]{0,1:T(4,128)S(1)}, f32[4,2048,128]{2,1,0:T(8,128)S(1)}) fusion(bf16[16,4,8,128]{3,2,1,0:T(8,128)(2,1)S(1)} %fusion.16, bf16[2048,512]{1,0:T(8,128)(2,1)} %all-gather.9.cloned.1.call-done), kind=kOutput, calls=%fused_computation.1 | convolution fusion | flops 270532096 | bytes 6424576 | tf_op jit(solution)/shard_map/while/body/eval_jaxpr/thd,rhd->thr/dot_general | solution.py:94
  104.5 0.0 copy-start.1
  104.5 0.7 fusion.1
  105.2 1.2 copy-done.1
  106.4 38.7 %all-gather.11.cloned.1.call-done = bf16[2048,512]{1,0:T(8,128)(2,1)} async-done(((bf16[128,512]{1,0:T(8,128)(2,1)}), bf16[2048,512]{1,0:T(8,128)(2,1)}) %all-gather.11.cloned.1.call-update) | async-done | bytes 2097168 | tf_op jit(solution)/shard_map/all_gather | solution.py:117
  145.1 4.0 %copy.29 = bf16[2048,512]{0,1:T(8,128)(2,1)} copy(bf16[2048,512]{1,0:T(8,128)(2,1)} %all-gather.11.cloned.1.call-done) | data formatting | bytes 4194304 | tf_op jit(solution)/shard_map/while/body/jit(dynamic_index_in_dim)/squeeze | solution.py:126
  149.1 4.0 %fusion.20 = bf16[128,4,128]{0,2,1:T(8,128)(2,1)S(1)} fusion(bf16[2048,4,128]{0,2,1:T(8,128)(2,1)} %bitcast.108, f32[4,2048,128]{2,1,0:T(8,128)} %copy-done.1, f32[128,4]{0,1:T(4,128)S(1)} %broadcast_maximum_fusion, f32[128,4]{0,1:T(4,128)S(1)} %get-tuple-element.46, f32[128,4]{0,1:T(4,128)S(1)} %get-tuple-element.38), kind=kOutput, calls=%fused_computation.23 | convolution fusion | flops 271777792 | bytes 6428672 | tf_op jit(solution)/shard_map/while/body/eval_jaxpr/thr,rhd->thd/dot_general | solution.py:101
  153.1 0.0 copy-done
  153.1 1.3 convolution_convert_fusion
  154.3 0.0 reduce-scatter.2.cloned.1.call-update
  154.4 1.8 %dynamic-slice_convert_fusion = bf16[128,1024]{1,0:T(8,128)(2,1)} fusion(f32[128,2048]{1,0:T(8,128)} %copy-done.2, s32[]{:T(128)S(6)} %select_n.12), kind=kLoop, calls=%fused_computation.30 | loop fusion | bytes 524292 | tf_op jit(solution)/shard_map/convert_element_type | solution.py:83
  156.2 11.7 %reduce-scatter.2.cloned.1.call-done = bf16[128,1024]{1,0:T(8,128)(2,1)} async-done(((bf16[128,2048]{1,0:T(8,128)(2,1)}), bf16[128,1024]{1,0:T(8,128)(2,1)}) %reduce-scatter.2.cloned.1.call-update) | async-done | bytes 262160 | tf_op jit(solution)/shard_map/reduce_scatter | solution.py:132
  (5 shorter events, 0.0 us)
Async XLA Ops:
  7.2 145.9 %copy-start = (bf16[512,2048]{1,0:T(8,128)(2,1)S(1)}, bf16[512,2048]{1,0:T(8,128)(2,1)}, u32[]{:S(2)}) copy-start(bf16[512,2048]{1,0:T(8,128)(2,1)} %param.23) | copy-start | bytes 6291460
  7.2 10.0 %copy-start.4 = (bf16[64,2048]{1,0:T(8,128)(2,1)S(1)}, bf16[64,2048]{1,0:T(8,128)(2,1)}, u32[]{:S(2)}) copy-start(bf16[64,2048]{1,0:T(8,128)(2,1)} %param.14) | copy-start | bytes 786436
  7.2 47.6 %all-gather.13.cloned.1.call-start = ((), (), s32[]{:S(2)}) async-start(), calls=%async_computation.4 | async-start | bytes 3145728 | tf_op jit(solution)/shard_map/all_gather | solution.py:11
  15.6 39.2 %copy-start.6 = (s32[128]{0:T(128)S(1)}, s32[128]{0:T(128)}, u32[]{:S(2)}) copy-start(s32[128]{0:T(128)} %param.17) | copy-start | bytes 1540
  18.8 83.3 %all-gather.9.cloned.1.call-start = ((), (), s32[]{:S(2)}) async-start(), calls=%async_computation.1 | async-start | bytes 2228224 | tf_op jit(solution)/shard_map/all_gather | solution.py:116
  54.8 3.6 %copy-start.5 = (f32[2048]{0:T(1024)S(1)}, f32[2048]{0:T(1024)}, u32[]{:S(2)}) copy-start(f32[2048]{0:T(1024)} %param.19) | copy-start | bytes 24580
  57.4 1.1 copy-start.2
  57.4 2.0 %copy-start.3 = (bf16[2048,512]{1,0:T(8,128)(2,1)S(1)}, bf16[2048,512]{1,0:T(8,128)(2,1)}, u32[]{:S(2)}) copy-start(bf16[2048,512]{1,0:T(8,128)(2,1)} %param.21) | copy-start | bytes 6291460
  60.5 84.6 %all-gather.11.cloned.1.call-start = ((), (), s32[]{:S(2)}) async-start(), calls=%async_computation.2 | async-start | bytes 2228224 | tf_op jit(solution)/shard_map/all_gather | solution.py:117
  63.2 104.6 %reduce-scatter.2.cloned.1.call-start = ((), (), s32[]{:S(2)}) async-start(), calls=%async_computation.3 | async-start | bytes 786432 | tf_op jit(solution)/shard_map/reduce_scatter | solution.py:132
  104.5 1.9 %copy-start.1 = (f32[4,2048,128]{2,1,0:T(8,128)}, f32[4,2048,128]{2,1,0:T(8,128)S(1)}, u32[]{:S(2)}) copy-start(f32[4,2048,128]{2,1,0:T(8,128)S(1)} %get-tuple-element.50) | copy-start | bytes 12582916
Sparse Core Ops, SparseCore 0:
  18.9 35.8 all-gather.12
  60.6 41.4 all-gather.8
  104.9 40.1 all-gather.10
  154.5 13.3 reduce-scatter.1
where the time goes:
time: 175 us; the launch traced here: 174 us
  waiting for transfers between devices  114 us (65%)
  matrix products  24.9 us (14%)
  between operations  13.9 us (8%)
  local copies, waits for them, and re-layouts  10.1 us (6%)
  blocking collectives  9.39 us (5%)
  other arithmetic  2.26 us (1%)
    all_gather x1, waiting for transfers between devices, on_device(): value_rows = lax.all_gather(values, 'blk', axis=0, tiled=True)  38.7 us
    all_gather x1, waiting for transfers between devices, on_device(): key_rows = lax.all_gather(keys, 'blk', axis=0, tiled=True)  36.8 us
    all_gather x1, waiting for transfers between devices, merged(): gathered = jax.tree.map(lambda a: lax.all_gather(a, axis), part)  26.5 us
    reduce_scatter x1, waiting for transfers between devices, on_device(): lax.psum_scatter(partial_value.astype(jnp.bfloat16), 'segment', scatter_d...  11.7 us
    all_gather x2, blocking collectives, merged(): gathered = jax.tree.map(lambda a: lax.all_gather(a, axis), part)  9.39 us
    unnamed x16, local copies, waits for them, and re-layouts  4.29 us
    squeeze x1, local copies, waits for them, and re-layouts, on_device(): carry, unused = lax.scan(one_block, carry, (key_blocks, value_blocks))  3.99 us
    dot_general x1, matrix products, attend(): jnp.einsum('thr,rhd->thd', expo.astype(jnp.bfloat16), value_heads, prefer...  3.99 us
  transfers between devices with their start and end apart: 4, of which 4 were waited for; matrix products, arithmetic and copies ran while one was open for 5% of the time, Pallas kernels for 0%

commit v1 on v0

--- a/solution.py
+++ b/solution.py
@@ -5,6 +5,24 @@
 from jax.sharding import PartitionSpec as P
 
 HEAD_DIM = 128
+
+
+def laid_out(tiles, dim):
+    dims = list(tiles.shape[1:])
+    dims[dim] *= tiles.shape[0]
+    return jnp.moveaxis(tiles, 0, dim).reshape(dims)
+
+
+def doubled(array, axis):
+    size = lax.axis_size(axis)
+    blocks = array[None]
+    for level in range(size.bit_length() - 1):
+        distance = 1 << level
+        theirs = lax.ppermute(blocks, axis, [(i, i ^ distance) for i in range(size)])
+        both = jnp.stack([blocks, theirs])
+        upper = lax.axis_index(axis) >> level & 1
+        blocks = jnp.where(upper == 0, both, both[::-1]).reshape(-1, *array.shape)
+    return blocks
 
 
 def merged(part, axis, combine):
@@ -113,7 +131,7 @@
         jnp.zeros((tok_rows, head_count, HEAD_DIM), jnp.float32),
     )
     carry = start_state
-    key_rows = lax.all_gather(keys, "blk", axis=0, tiled=True)
+    key_rows = laid_out(doubled(keys, "blk"), 0)
     value_rows = lax.all_gather(values, "blk", axis=0, tiled=True)
     rows = key_rows.shape[0]
     block = 2048

time: 175 us -> 190 us (1.086)
  local copies, waits for them, and re-layouts: 10.1 us -> 16.7 us
  other arithmetic: 2.26 us -> 8.3 us
  starting transfers between devices: 0.16 us -> 5.7 us
  waiting for transfers between devices: 114 us -> 111 us
    ppermute x0 -> x4, waiting for transfers between devices: none -> 72.3 us  [doubled(): lax.ppermute(blocks, axis, [(i, i ^ distance) for i in range(size)])]
    all_gather x1, waiting for transfers between devices: 38.7 us -> 0.01 us  [on_device(): value_rows = lax.all_gather(values, 'blk', axis=0, tiled=True)]
    all_gather x1 -> x0, waiting for transfers between devices: 36.8 us -> none  [on_device(): key_rows = lax.all_gather(keys, 'blk', axis=0, tiled=True)]
    ppermute x0 -> x4, starting transfers between devices: none -> 5.58 us  [doubled(): lax.ppermute(blocks, axis, [(i, i ^ distance) for i in range(size)])]
    squeeze x1 -> x2, local copies, waits for them, and re-layouts: 3.99 us -> 8.13 us  [on_device(): carry, unused = lax.scan(one_block, carry, (key_blocks, value_blocks))]
    select_n x0 -> x3, other arithmetic: none -> 3.2 us  [doubled(): blocks = jnp.where(upper == 0, both, both[::-1]).reshape(-1, *array.shape)]
    another operation x0 -> x5, other arithmetic: none -> 2.84 us  [doubled(): both = jnp.stack([blocks, theirs])]
    select_n x0 -> x1, local copies, waits for them, and re-layouts: none -> 2.45 us  [doubled(): blocks = jnp.where(upper == 0, both, both[::-1]).reshape(-1, *array.shape)]
  transfers between devices with their start and end apart: 4 -> 7, of which waited for: 4 -> 6; matrix products, arithmetic and copies ran while one was open for 5% -> 12% of each run, Pallas kernels for 0% -> 0%
where the time goes in v1:
time: 190 us; the launch traced here: 189 us
  waiting for transfers between devices  111 us (58%)
  matrix products  24.4 us (13%)
  local copies, waits for them, and re-layouts  16.7 us (9%)
  between operations  13.9 us (7%)
  blocking collectives  9.38 us (5%)
  other arithmetic  8.3 us (4%)
  starting transfers between devices  5.7 us (3%)
    ppermute x4, waiting for transfers between devices, doubled(): lax.ppermute(blocks, axis, [(i, i ^ distance) for i in range(size)])  72.3 us
    all_gather x1, waiting for transfers between devices, merged(): gathered = jax.tree.map(lambda a: lax.all_gather(a, axis), part)  26.5 us
    reduce_scatter x1, waiting for transfers between devices, on_device(): lax.psum_scatter(partial_value.astype(jnp.bfloat16), 'segment', scatter_d...  12.1 us
    all_gather x2, blocking collectives, merged(): gathered = jax.tree.map(lambda a: lax.all_gather(a, axis), part)  9.38 us
    squeeze x2, local copies, waits for them, and re-layouts, on_device(): carry, unused = lax.scan(one_block, carry, (key_blocks, value_blocks))  8.13 us
    ppermute x4, starting transfers between devices, doubled(): lax.ppermute(blocks, axis, [(i, i ^ distance) for i in range(size)])  5.58 us
    unnamed x18, local copies, waits for them, and re-layouts  4.29 us
    dot_general x1, matrix products, attend(): jnp.einsum('thr,rhd->thd', expo.astype(jnp.bfloat16), value_heads, prefer...  3.98 us
  transfers between devices with their start and end apart: 7, of which 6 were waited for; matrix products, arithmetic and copies ran while one was open for 12% of the time, Pallas kernels for 0%

profile of v1, /device:TPU:0, one launch (start us, length us, event | category | flops | bytes accessed | tf_op | source)
XLA Modules:
  0.0 189.3 jit_solution(16521656248652557285)
XLA Ops:
  7.2 0.0 copy-start
  7.2 0.0 copy-start.5
  7.2 0.0 all-gather.10.cloned.1.call-start
  7.2 0.9 reshape.129
  8.1 0.7 reshape.125
  8.8 1.1 convolution_bitcast_fusion.1
  9.9 1.6 fusion.48
  11.5 0.9 fusion.33
  12.4 1.2 fusion.49
  13.6 0.1 fusion.31
  13.7 0.1 fusion.46
  13.8 0.9 convert_multiply_fusion
  14.7 0.8 fusion.28
  15.5 0.0 copy-start.7
  15.5 1.5 convolution_bitcast_fusion
  17.0 0.0 copy-done.5
  17.1 1.6 convolution_add_fusion.1
  18.7 0.0 all-gather.10.cloned.1.call-update
  18.7 0.0 all-gather.8.cloned.1.call-start
  18.8 5.2 %all-gather.4 = f32[2,1,128]{2,1,0:T(1,128)S(1)} all-gather(f32[1,1,128]{2,1,0:T(1,128)S(1)} %bitcast.132), channel_id=4, replica_groups=mesh['segment'=2,'blk'=16] {'segment'}, dimensions={0}, use_global_device_ids=true | all-gather | bytes 1536 | tf_op jit(solution)/shard_map/all_gather | solution.py:29
  23.9 4.2 %all-gather.3 = f32[2,1,128]{2,1,0:T(1,128)S(1)} all-gather(f32[1,1,128]{2,1,0:T(1,128)S(1)} %bitcast.131), channel_id=3, replica_groups=mesh['segment'=2,'blk'=16] {'segment'}, dimensions={0}, use_global_device_ids=true | all-gather | bytes 1536 | tf_op jit(solution)/shard_map/all_gather | solution.py:29
  28.2 26.5 %all-gather.10.cloned.1.call-done = f32[256,2048]{1,0:T(8,128)} async-done(((f32[128,2048]{1,0:T(8,128)}), f32[256,2048]{1,0:T(8,128)}) %all-gather.10.cloned.1.call-update) | async-done | bytes 2097168 | tf_op jit(solution)/shard_map/all_gather | solution.py:29
  54.7 0.0 copy-done.7
  54.7 0.0 copy-start.6
  54.7 2.6 %fusion.47 = (f32[128]{0:T(128)S(1)}, f32[128,2048]{1,0:T(8,128)S(1)}) fusion(bf16[360,2048]{1,0:T(8,128)(2,1)} %param.18, s32[128]{0:T(128)S(1)} %copy-done.7, f32[128]{0:T(128)S(1)} %get-tuple-element.33, f32[128]{0:T(128)S(1)} %get-tuple-element.35, f32[256,2048]{1,0:T(8,128)} %all-gather.10.cloned.1.call-done, f32[128]{0:T(128)S(1)} %get-tuple-element.34), kind=kOutput, calls=%fused_computation.73 | convolution fusion | flops 190362496 | bytes 4622848 | tf_op jit(solution)/shard_map/dot_general | solution.py:95
  57.3 0.0 copy-start.4
  57.3 0.3 multiply_reduce_fusion
  57.6 0.0 copy-done.6
  57.6 0.2 multiply_convert_fusion
  57.8 1.5 copy-done.4
  59.3 0.4 convolution_convert_fusion.3
  59.7 0.0 copy-done.2
  59.7 0.1 collective-permute-start
  59.8 1.3 collective-permute-done
  61.2 0.1 fusion.23
  61.2 1.5 collective-permute-start.1
  62.8 2.7 %convolution_convert_fusion.1 = bf16[128,512]{1,0:T(8,128)(2,1)} fusion(bf16[128,2048]{1,0:T(8,128)(2,1)S(1)} %multiply_convert_fusion, bf16[2048,512]{1,0:T(8,128)(2,1)} %param.22), kind=kOutput, calls=%fused_computation.17 | convolution fusion | flops 268500992 | bytes 2752512 | tf_op jit(solution)/shard_map/dot_general | solution.py:104
  65.5 0.0 all-gather.8.cloned.1.call-update
  65.5 0.0 reduce-scatter.2.cloned.1.call-start
  65.6 4.1 %collective-permute-done.1 = bf16[2,128,512]{2,1,0:T(8,128)(2,1)S(1)} collective-permute-done((bf16[2,128,512]{2,1,0:T(8,128)(2,1)S(1)}, bf16[2,128,512]{2,1,0:T(8,128)(2,1)S(1)}, u32[]{:S(2)}, u32[]{:S(2)}) %collective-permute-start.1) | collective-permute-done | bytes 262176 | tf_op jit(solution)/shard_map/ppermute | solution.py:21
  69.7 0.1 pad_maximum_fusion.2
  69.7 0.1 reverse_select_fusion.2
  69.8 1.6 collective-permute-start.2
  71.4 16.0 %collective-permute-done.2 = bf16[4,128,512]{2,1,0:T(8,128)(2,1)} collective-permute-done((bf16[4,128,512]{2,1,0:T(8,128)(2,1)S(1)}, bf16[4,128,512]{2,1,0:T(8,128)(2,1)}, u32[]{:S(2)}, u32[]{:S(2)}) %collective-permute-start.2) | collective-permute-done | bytes 524320 | tf_op jit(solution)/shard_map/ppermute | solution.py:21
  87.3 1.1 pad_maximum_fusion.1
  88.5 1.2 reverse_select_fusion.1
  89.7 2.4 %copy.27 = bf16[2,4,128,512]{2,1,0,3:T(4,128)(2,1)} copy(bf16[2,4,128,512]{3,2,1,0:T(8,128)(2,1)} %reverse_select_fusion.1) | data formatting | bytes 2097152 | tf_op jit(solution)/shard_map/jit(_where)/select_n | solution.py:24
  92.1 2.4 %collective-permute-start.3 = (bf16[8,128,512]{1,0,2:T(8,128)(2,1)}, bf16[8,128,512]{1,0,2:T(8,128)(2,1)}, u32[]{:S(2)}, u32[]{:S(2)}) collective-permute-start(bf16[8,128,512]{1,0,2:T(8,128)(2,1)} %bitcast.117), channel_id=1, source_target_pairs={{0,8},{1,9},{2,10},{3,11},{4,12},{5,13},{6,14},{7,15},{8,0},{9,1},... | collective-permute-start | bytes 3145736 | tf_op jit(solution)/shard_map/ppermute | solution.py:21
  94.5 2.1 %fusion.13 = bf16[16,4,8,128]{3,2,1,0:T(8,128)(2,1)S(1)} fusion(bf16[128,2048]{1,0:T(8,128)(2,1)S(1)} %multiply_convert_fusion, bf16[2048,512]{1,0:T(8,128)(2,1)} %param.20), kind=kOutput, calls=%fused_computation.20 | convolution fusion | flops 268500992 | bytes 2752512 | tf_op jit(solution)/shard_map/dot_general | solution.py:102
  96.7 50.9 %collective-permute-done.3 = bf16[8,128,512]{1,0,2:T(8,128)(2,1)} collective-permute-done((bf16[8,128,512]{1,0,2:T(8,128)(2,1)}, bf16[8,128,512]{1,0,2:T(8,128)(2,1)}, u32[]{:S(2)}, u32[]{:S(2)}) %collective-permute-start.3) | collective-permute-done | bytes 1048608 | tf_op jit(solution)/shard_map/ppermute | solution.py:21
  147.5 0.0 copy-done.3
  147.5 1.6 pad_maximum_fusion
  149.1 1.9 %reverse_select_fusion = bf16[2,8,128,512]{2,1,0,3:T(8,128)(2,1)} fusion(bf16[2,8,128,512]{2,1,0,3:T(8,128)(2,1)S(1)} %pad_maximum_fusion, pred[]{:T(512)S(6)} %eq.44), kind=kLoop, calls=%fused_computation.5 | loop fusion | flops 1048576 | bytes 4194305 | tf_op jit(solution)/shard_map/jit(_where)/select_n | solution.py:24
  151.0 4.2 %squeeze.38 = bf16[2048,4,128]{0,2,1:T(8,128)(2,1)} reshape(bf16[2,8,128,512]{2,1,0,3:T(8,128)(2,1)} %reverse_select_fusion) | data formatting | bytes 4194304 | tf_op jit(solution)/shard_map/while/body/jit(dynamic_index_in_dim)/squeeze | solution.py:144
  155.2 2.5 %bitcast_reduce_fusion = (f32[128,4]{0,1:T(4,128)S(1)}, f32[4,2048,128]{2,1,0:T(8,128)S(1)}) fusion(bf16[2048,4,128]{0,2,1:T(8,128)(2,1)} %squeeze.38, bf16[16,4,8,128]{3,2,1,0:T(8,128)(2,1)S(1)} %fusion.13), kind=kOutput, calls=%fused_computation.1 | convolution fusion | flops 270532096 | bytes 6424576 | tf_op jit(solution)/shard_map/while/body/eval_jaxpr/thd,rhd->thr/dot_general | solution.py:112
  157.7 0.7 fusion.1
  158.4 1.2 copy-done.1
  159.7 4.0 %copy.38 = bf16[2048,512]{0,1:T(8,128)(2,1)} copy(bf16[2048,512]{1,0:T(8,128)(2,1)} %all-gather.8.cloned.1.call-done) | data formatting | bytes 4194304 | tf_op jit(solution)/shard_map/while/body/jit(dynamic_index_in_dim)/squeeze | solution.py:144
  163.6 4.0 %fusion.17 = bf16[128,4,128]{0,2,1:T(8,128)(2,1)S(1)} fusion(bf16[2048,4,128]{0,2,1:T(8,128)(2,1)} %bitcast.119, f32[4,2048,128]{2,1,0:T(8,128)} %copy-done.1, f32[128,4]{0,1:T(4,128)S(1)} %broadcast_maximum_fusion, f32[128,4]{0,1:T(4,128)S(1)} %get-tuple-element.48, f32[128,4]{0,1:T(4,128)S(1)} %get-tuple-element.47), kind=kOutput, calls=%fused_computation.23 | convolution fusion | flops 271777792 | bytes 6428672 | tf_op jit(solution)/shard_map/while/body/eval_jaxpr/thr,rhd->thd/dot_general | solution.py:119
  167.6 0.0 copy-done
  167.6 1.3 convolution_convert_fusion
  168.9 0.0 reduce-scatter.2.cloned.1.call-update
  168.9 1.8 dynamic-slice_convert_fusion
  170.7 12.1 %reduce-scatter.2.cloned.1.call-done = bf16[128,1024]{1,0:T(8,128)(2,1)} async-done(((bf16[128,2048]{1,0:T(8,128)(2,1)}), bf16[128,1024]{1,0:T(8,128)(2,1)}) %reduce-scatter.2.cloned.1.call-update) | async-done | bytes 262160 | tf_op jit(solution)/shard_map/reduce_scatter | solution.py:150
  (10 shorter events, 0.1 us)
Async XLA Ops:
  7.2 160.5 %copy-start = (bf16[512,2048]{1,0:T(8,128)(2,1)S(1)}, bf16[512,2048]{1,0:T(8,128)(2,1)}, u32[]{:S(2)}) copy-start(bf16[512,2048]{1,0:T(8,128)(2,1)} %param.23) | copy-start | bytes 6291460
  7.2 9.9 %copy-start.5 = (bf16[64,2048]{1,0:T(8,128)(2,1)S(1)}, bf16[64,2048]{1,0:T(8,128)(2,1)}, u32[]{:S(2)}) copy-start(bf16[64,2048]{1,0:T(8,128)(2,1)} %param.14) | copy-start | bytes 786436
  7.2 47.5 %all-gather.10.cloned.1.call-start = ((), (), s32[]{:S(2)}) async-start(), calls=%async_computation.3 | async-start | bytes 3145728 | tf_op jit(solution)/shard_map/all_gather | solution.py:29
  15.5 39.2 %copy-start.7 = (s32[128]{0:T(128)S(1)}, s32[128]{0:T(128)}, u32[]{:S(2)}) copy-start(s32[128]{0:T(128)} %param.17) | copy-start | bytes 1540
  18.7 141.0 %all-gather.8.cloned.1.call-start = ((), (), s32[]{:S(2)}) async-start(), calls=%async_computation.1 | async-start | bytes 2228224 | tf_op jit(solution)/shard_map/all_gather | solution.py:135
  54.7 2.9 %copy-start.6 = (f32[2048]{0:T(1024)S(1)}, f32[2048]{0:T(1024)}, u32[]{:S(2)}) copy-start(f32[2048]{0:T(1024)} %param.19) | copy-start | bytes 24580
  57.3 2.4 %copy-start.2 = (f32[128,2048]{1,0:T(8,128)}, f32[128,2048]{1,0:T(8,128)S(1)}, u32[]{:S(2)}) copy-start(f32[128,2048]{1,0:T(8,128)S(1)} %get-tuple-element.50) | copy-start | bytes 3145732
  57.3 2.0 %copy-start.4 = (bf16[2048,512]{1,0:T(8,128)(2,1)S(1)}, bf16[2048,512]{1,0:T(8,128)(2,1)}, u32[]{:S(2)}) copy-start(bf16[2048,512]{1,0:T(8,128)(2,1)} %param.21) | copy-start | bytes 6291460
  59.7 1.4 collective-permute-start
  61.2 8.4 %collective-permute-start.1 = (bf16[2,128,512]{2,1,0:T(8,128)(2,1)S(1)}, bf16[2,128,512]{2,1,0:T(8,128)(2,1)S(1)}, u32[]{:S(2)}, u32[]{:S(2)}) collective-permute-start(bf16[2,128,512]{2,1,0:T(8,128)(2,1)S(1)} %get-tuple-element.46), channel_id=1, source_target_pairs={{0,2},{1,3},{2,0},{3,1},{4,6},{5,7},{6,4},{7,5},{8,10},{9,11},{10,... | collective-permute-start | bytes 786440 | tf_op jit(solution)/shard_map/ppermute | solution.py:21
  65.5 117.3 %reduce-scatter.2.cloned.1.call-start = ((), (), s32[]{:S(2)}) async-start(), calls=%async_computation.2 | async-start | bytes 786432 | tf_op jit(solution)/shard_map/reduce_scatter | solution.py:150
  69.8 17.5 %collective-permute-start.2 = (bf16[4,128,512]{2,1,0:T(8,128)(2,1)S(1)}, bf16[4,128,512]{2,1,0:T(8,128)(2,1)}, u32[]{:S(2)}, u32[]{:S(2)}) collective-permute-start(bf16[4,128,512]{2,1,0:T(8,128)(2,1)S(1)} %bitcast.120), channel_id=1, source_target_pairs={{0,4},{1,5},{2,6},{3,7},{4,0},{5,1},{6,2},{7,3},{8,12},{9,13},{10,... | collective-permute-start | bytes 1572872 | tf_op jit(solution)/shard_map/ppermute | solution.py:21
  92.1 55.4 %collective-permute-start.3 = (bf16[8,128,512]{1,0,2:T(8,128)(2,1)}, bf16[8,128,512]{1,0,2:T(8,128)(2,1)}, u32[]{:S(2)}, u32[]{:S(2)}) collective-permute-start(bf16[8,128,512]{1,0,2:T(8,128)(2,1)} %bitcast.117), channel_id=1, source_target_pairs={{0,8},{1,9},{2,10},{3,11},{4,12},{5,13},{6,14},{7,15},{8,0},{9,1},... | collective-permute-start | bytes 3145736 | tf_op jit(solution)/shard_map/ppermute | solution.py:21
  94.5 53.0 %copy-start.3 = (bf16[2,4,128,512]{2,1,0,3:T(4,128)(2,1)S(1)}, bf16[2,4,128,512]{2,1,0,3:T(4,128)(2,1)}, u32[]{:S(2)}) copy-start(bf16[2,4,128,512]{2,1,0,3:T(4,128)(2,1)} %copy.27) | copy-start | bytes 3145732
  157.7 1.9 %copy-start.1 = (f32[4,2048,128]{2,1,0:T(8,128)}, f32[4,2048,128]{2,1,0:T(8,128)S(1)}, u32[]{:S(2)}) copy-start(f32[4,2048,128]{2,1,0:T(8,128)S(1)} %get-tuple-element.52) | copy-start | bytes 12582916
Sparse Core Ops, SparseCore 0:
  18.8 35.7 all-gather.9
  65.6 65.0 all-gather.7
  169.0 13.7 reduce-scatter.1
